TPU v7x, 32 devices: a whole 2x2x4 slice. The times are simulated.
32 devices in a mesh: group: 2 (over y), clip: 4 (over x, core), seq: 4 (over z).
Axes of the slice: x: 2, y: 2, z: 4, core: 2. Of those that a mesh axis runs over, the one named last changes fastest.
Arguments:
- queries: bfloat16 [8, 512, 2048], P(('group', 'clip'), 'seq'), parts along dimension 0, may hold values from -18 to 18
- key_states: bfloat16 [8, 512, 2048], P(('group', 'clip'), 'seq'), parts along dimension 0, may hold values from -18 to 18
- value_states: bfloat16 [8, 512, 2048], P(('group', 'clip'), 'seq'), parts along dimension 0, may hold values from -6 to 6
- query_tangent: bfloat16 [8, 512, 2048], P(('group', 'clip'), 'seq'), parts along dimension 0, may hold values from -6 to 6
- key_tangent: bfloat16 [8, 512, 2048], P(('group', 'clip'), 'seq'), parts along dimension 0, may hold values from -6 to 6
- value_tangent: bfloat16 [8, 512, 2048], P(('group', 'clip'), 'seq'), parts along dimension 0, may hold values from -6 to 6
- offsets: int32 [8], P(('group', 'clip')), parts along dimension 0, may hold values from 0 to 130560
Outputs:
- attended: bfloat16 [8, 512, 2048], P(('group', 'clip'), 'seq'), parts along dimension 0
- attended_tangent: bfloat16 [8, 512, 2048], P(('group', 'clip'), 'seq'), parts along dimension 0
There are 2 independent parts, one for each index of `group`. A program takes and returns all parts, laid end to end along the dimension named above; each array names one. Nothing has to cross between parts.
All inputs are finite; a program needn't handle non-finite values.
Results may differ from a plain program's by a relative error of at most 0.012.
The roundings to bfloat16 on the way count: a program that leaves them out, or rounds other values in their place, can miss the bound.
Values may be sent and summed in bfloat16 or wider, within the bound.
No kernel may reach another device: no remote copies, remote signals or barrier semaphores. Data moves between devices by JAX's collectives and lax.ppermute only.
A program may use at most 64 MiB of HBM per device.

v0:
```python
import math
import jax
import jax.numpy as jnp
from jax import lax
from jax.sharding import PartitionSpec as P

H = 16
HD = 128
HH = 44
WW = 80
rope_theta = 10000.0


def rope_tables(first, count):
    global_index = first + jnp.arange(count, dtype=jnp.int32)
    frames = global_index // (HH * WW)
    grid_row = global_index // WW % HH
    column = global_index % WW
    spatial = HD // 6 * 2
    temporal = HD - 2 * spatial
    channel = jnp.arange(HD, dtype=jnp.int32)
    part_start = jnp.where(
        channel < temporal, 0, jnp.where(channel < temporal + spatial, temporal, temporal + spatial)
    )
    extent = jnp.where(channel < temporal, temporal, spatial)
    pair_index = (channel - part_start) // 2
    frequency = jnp.exp(
        -(2.0 * pair_index.astype(jnp.float32) / extent.astype(jnp.float32)) * math.log(rope_theta)
    )
    position = jnp.where(
        channel[None, :] < temporal,
        frames[:, None],
        jnp.where(channel[None, :] < temporal + spatial, grid_row[:, None], column[:, None]),
    )
    angles = position.astype(jnp.float32) * frequency[None, :]
    return (jnp.cos(angles)[:, None, :], jnp.sin(angles)[:, None, :])


def rotate(tensor, cosine, sine):
    channel = jnp.arange(tensor.shape[-1], dtype=jnp.int32)
    partner = jnp.where(
        channel % 2 == 0, -jnp.roll(tensor, -1, axis=-1), jnp.roll(tensor, 1, axis=-1)
    )
    return (tensor * cosine + partner * sine).astype(jnp.bfloat16)


def primal_terms(query_blk, keys_all, values_all, scaling):
    scores = (
        jnp.einsum("bhd,khd->hbk", query_blk, keys_all, preferred_element_type=jnp.float32)
        * scaling
    )
    largest = jnp.max(scores, axis=-1, keepdims=True)
    expons = jnp.exp(scores - largest)
    probs = expons / jnp.sum(expons, axis=-1, keepdims=True)
    weights = probs.astype(jnp.bfloat16)
    out_full = jnp.einsum("hbk,khd->bhd", weights, values_all, preferred_element_type=jnp.float32)
    return (weights, out_full)


def tangent_terms(
    query_blk, qdot_blk, keys_all, kdots_all, values_all, vdots_all, weights, out_full, scaling
):
    scores_dot = (
        jnp.einsum("bhd,khd->hbk", qdot_blk, keys_all, preferred_element_type=jnp.float32)
        + jnp.einsum("bhd,khd->hbk", query_blk, kdots_all, preferred_element_type=jnp.float32)
    ) * scaling
    product = weights.astype(jnp.float32) * scores_dot
    correction = jnp.sum(product, axis=-1)
    product_half = product.astype(jnp.bfloat16)
    tangent = (
        jnp.einsum("hbk,khd->bhd", weights, vdots_all, preferred_element_type=jnp.float32)
        + jnp.einsum("hbk,khd->bhd", product_half, values_all, preferred_element_type=jnp.float32)
        - jnp.transpose(correction)[:, :, None] * out_full
    )
    return tangent.astype(jnp.bfloat16)


def body(queries, key_states, value_states, query_tangent, key_tangent, value_tangent, offsets):
    devices = lax.axis_size("seq")
    repeat = max(devices // H, 1)
    per_device = max(H // devices, 1)
    groups = H // per_device
    width = per_device * HD
    tokens = queries.shape[1]
    sub_rows = tokens // repeat
    scaling = 1.0 / math.sqrt(HD)
    first = offsets[0] + lax.axis_index("seq") * tokens
    cosine, sine = rope_tables(first, tokens)

    def roped(array):
        return rotate(array[0].reshape(tokens, H, HD).astype(jnp.float32), cosine, sine).reshape(
            tokens, H * HD
        )

    def by_rows(array):
        shaped = array.reshape(repeat, sub_rows, groups, width)
        return jnp.transpose(shaped, (2, 0, 1, 3)).reshape(devices, sub_rows, width)

    def by_copies(array):
        shaped = jnp.transpose(array.reshape(tokens, groups, width), (1, 0, 2))
        spread = jnp.broadcast_to(shaped[:, None], (groups, repeat, tokens, width))
        return spread.reshape(devices, tokens, width)

    query_send = by_rows(roped(queries))
    qdot_send = by_rows(roped(query_tangent))
    key_send = by_copies(roped(key_states))
    kdot_send = by_copies(roped(key_tangent))
    value_send = by_copies(value_states[0])
    vdot_send = by_copies(value_tangent[0])
    query_rows = devices * sub_rows
    block = min(512, query_rows)
    count = query_rows // block

    def heads_view(array):
        return array.reshape(array.shape[0], per_device, HD)

    def blocks(array):
        return array.reshape(count, block, per_device, HD)

    received = (
        lax.all_to_all(query_send, "seq", split_axis=0, concat_axis=1, tiled=True),
        lax.all_to_all(key_send, "seq", split_axis=0, concat_axis=1, tiled=True),
        lax.all_to_all(value_send, "seq", split_axis=0, concat_axis=1, tiled=True),
        lax.all_to_all(qdot_send, "seq", split_axis=0, concat_axis=1, tiled=True),
        lax.all_to_all(kdot_send, "seq", split_axis=0, concat_axis=1, tiled=True),
        lax.all_to_all(vdot_send, "seq", split_axis=0, concat_axis=1, tiled=True),
    )
    query_in, key_in, value_in, qdot_in, kdot_in, vdot_in = tuple((array[0] for array in received))
    keys_all, values_all = (heads_view(key_in), heads_view(value_in))
    kdots_all, vdots_all = (heads_view(kdot_in), heads_view(vdot_in))

    def one_block(parts):
        query_blk, qdot_blk = parts
        weights, out_full = primal_terms(query_blk, keys_all, values_all, scaling)
        tangent = tangent_terms(
            query_blk,
            qdot_blk,
            keys_all,
            kdots_all,
            values_all,
            vdots_all,
            weights,
            out_full,
            scaling,
        )
        return (out_full.astype(jnp.bfloat16), tangent)

    attended, tangent_out = lax.map(one_block, (blocks(query_in), blocks(qdot_in)))

    def to_sources(array):
        return array.reshape(devices, sub_rows, width)

    returned = (
        lax.all_to_all(to_sources(attended), "seq", split_axis=0, concat_axis=0, tiled=True),
        lax.all_to_all(to_sources(tangent_out), "seq", split_axis=0, concat_axis=0, tiled=True),
    )

    def to_tokens(array):
        shaped = array.reshape(groups, repeat, sub_rows, width)
        return jnp.transpose(shaped, (1, 2, 0, 3)).reshape(tokens, H * HD)[None]

    return (to_tokens(returned[0]), to_tokens(returned[1]))


def solution(mesh):
    in_specs = (
        P(("group", "clip"), "seq", None),
        P(("group", "clip"), "seq", None),
        P(("group", "clip"), "seq", None),
        P(("group", "clip"), "seq", None),
        P(("group", "clip"), "seq", None),
        P(("group", "clip"), "seq", None),
        P(("group", "clip")),
    )
    out_specs = (P(("group", "clip"), "seq", None), P(("group", "clip"), "seq", None))
    return jax.shard_map(body, mesh=mesh, in_specs=in_specs, out_specs=out_specs, check_vma=False)
```

profile of v0, /device:TPU:0, one launch (start us, length us, event | category | flops | bytes accessed | tf_op | source)
XLA Modules:
  0.0 167.7 jit_solution(8478201329883006545)
XLA Ops:
  0.6 1.3 copy.48
  1.9 1.5 fusion.48
  3.7 1.2 fusion.50
  5.7 1.9 %maximum_negate_fusion.2 = (f32[128,16,128]{0,2,1:T(8,128)S(1)}, f32[128,16,128]{0,2,1:T(8,128)S(1)}) fusion(f32[128,16,1]{0,2,1:T(1,128)S(1)} %get-tuple-element.40, f32[128,16,127]{0,2,1:T(8,128)} %get-tuple-element.42, f32[128,16,127]{0,2,1:T(8,128)} %get-tuple-element.41, f32[128,16,1]{0,2,1:T(1,128)S(1)} %get-tuple-element.39), kind=kLoop, calls=%fused_computation.26 | loop fusion | flops 786432 | bytes 4194304 | tf_op jit(solution)/shard_map/neg | solution.py:42
  8.4 1.8 %fusion.24 = (bf16[4,128,512]{1,2,0:T(8,128)(2,1)}, bf16[4,128,512]{1,2,0:T(8,128)(2,1)}) fusion(f32[1,128,4,512]{1,3,2,0:T(8,128)S(1)} %bitcast.120, f32[1,128,4,512]{1,3,2,0:T(8,128)S(1)} %bitcast.122, f32[1,128,4,512]{1,3,2,0:T(8,128)S(1)} %bitcast.123, f32[1,128,4,512]{1,3,2,0:T(8,128)S(1)} %bitcast.108, f32[1,128,4,512]{1,3,2,0:T(8,128)S(1)} %bitcast.118, ...), kind=kLoop, calls=%fused_computation.35 | loop fusion | flops 2621440 | bytes 9437696 | tf_op jit(solution)/shard_map/reshape | solution.py:97
  10.1 6.3 %all-to-all-start = ((bf16[4,128,512]{1,2,0:T(8,128)(2,1)}), bf16[4,128,512]{1,2,0:T(8,128)(2,1)}, u32[]{:S(2)}, u32[]{:S(2)}) async-start(bf16[4,128,512]{1,2,0:T(8,128)(2,1)} %get-tuple-element.25), calls=%async_computation | async-start | bytes 1048576 | tf_op jit(solution)/shard_map/all_to_all | solution.py:121
  16.5 1.2 copy.35
  17.7 1.5 fusion.51
  19.2 1.2 copy.53
  20.7 1.0 copy-done.6
  22.6 0.6 copy-done.1
  23.2 1.7 %fusion.25 = (bf16[4,128,512]{1,2,0:T(8,128)(2,1)}, bf16[4,128,512]{1,2,0:T(8,128)(2,1)}) fusion(f32[128,4,512]{0,2,1:T(8,128)S(1)} %bitcast.117, pred[512]{0:T(512)(128)(4,1)S(1)} %broadcast_bitcast_fusion, f32[128,4,512]{0,2,1:T(8,128)S(1)} %bitcast.114, f32[128,4,512]{0,2,1:T(8,128)S(1)} %bitcast.121, f32[128,4,512]{0,2,1:T(8,128)S(1)} %bitcast.129, ...), kind=kLoop, calls=%fused_computation.36 | loop fusion | flops 2621440 | bytes 9437696 | tf_op jit(solution)/shard_map/transpose | solution.py:100
  25.0 6.1 %all-to-all-done = bf16[4,128,512]{1,2,0:T(8,128)(2,1)} async-done(((bf16[4,128,512]{1,2,0:T(8,128)(2,1)}), bf16[4,128,512]{1,2,0:T(8,128)(2,1)}, u32[]{:S(2)}, u32[]{:S(2)}) %all-to-all-start) | async-done | bytes 524320 | tf_op jit(solution)/shard_map/all_to_all | solution.py:121
  31.1 17.5 %all_to_all.64 = bf16[4,128,512]{1,2,0:T(8,128)(2,1)S(1)} all-to-all(bf16[4,128,512]{1,2,0:T(8,128)(2,1)} %get-tuple-element.23), channel_id=1, replica_groups=mesh['group'=2,'clip'=4,'seq'=4] {'seq'}, dimensions={0} | all-to-all | bytes 1048576 | tf_op jit(solution)/shard_map/all_to_all | solution.py:122
  48.6 17.7 %all_to_all.65 = bf16[4,128,512]{1,2,0:T(8,128)(2,1)} all-to-all(bf16[4,128,512]{1,2,0:T(8,128)(2,1)} %get-tuple-element.24), channel_id=1, replica_groups=mesh['group'=2,'clip'=4,'seq'=4] {'seq'}, dimensions={0} | all-to-all | bytes 1048576 | tf_op jit(solution)/shard_map/all_to_all | solution.py:124
  66.3 3.5 %all-to-all-start.6 = ((bf16[4,128,512]{1,2,0:T(8,128)(2,1)}), bf16[4,128,512]{1,2,0:T(8,128)(2,1)S(1)}, u32[]{:S(2)}, u32[]{:S(2)}) async-start(bf16[4,128,512]{1,2,0:T(8,128)(2,1)} %get-tuple-element.22), calls=%async_computation.6 | async-start | bytes 1048576 | tf_op jit(solution)/shard_map/all_to_all | solution.py:125
  69.7 1.4 reshape_squeeze.25
  71.2 0.9 copy.94
  72.4 0.9 copy.93
  73.3 1.2 copy.34
  75.1 8.2 %all-to-all-done.6 = bf16[4,128,512]{1,2,0:T(8,128)(2,1)S(1)} async-done(((bf16[4,128,512]{1,2,0:T(8,128)(2,1)}), bf16[4,128,512]{1,2,0:T(8,128)(2,1)S(1)}, u32[]{:S(2)}, u32[]{:S(2)}) %all-to-all-start.6) | async-done | bytes 524320 | tf_op jit(solution)/shard_map/all_to_all | solution.py:125
  83.3 3.5 %all-to-all-start.2 = ((bf16[4,128,512]{2,1,0:T(8,128)(2,1)}), bf16[4,128,512]{2,1,0:T(8,128)(2,1)S(1)}, u32[]{:S(2)}, u32[]{:S(2)}) async-start(bf16[4,128,512]{2,1,0:T(8,128)(2,1)} %bitcast.100), calls=%async_computation.2 | async-start | bytes 1048576 | tf_op jit(solution)/shard_map/all_to_all | solution.py:123
  86.8 0.7 fusion.35
  87.5 3.1 %fusion.53 = (f32[4,512]{1,0:T(4,128)S(1)}, f32[4,512,512]{1,2,0:T(8,128)}) fusion(f32[4,512,512]{1,2,0:T(8,128)S(1)} %fusion.35), kind=kOutput, calls=%fused_computation.82 | output fusion | flops 4194815 | bytes 8396800 | tf_op jit(solution)/shard_map/while/body/eval_jaxpr/sub | solution.py:53
  90.6 10.2 %all-to-all-done.2 = bf16[4,128,512]{2,1,0:T(8,128)(2,1)S(1)} async-done(((bf16[4,128,512]{2,1,0:T(8,128)(2,1)}), bf16[4,128,512]{2,1,0:T(8,128)(2,1)S(1)}, u32[]{:S(2)}, u32[]{:S(2)}) %all-to-all-start.2) | async-done | bytes 524320 | tf_op jit(solution)/shard_map/all_to_all | solution.py:123
  100.8 4.3 %all-to-all-start.4 = ((bf16[4,128,512]{2,1,0:T(8,128)(2,1)}), bf16[4,128,512]{2,1,0:T(8,128)(2,1)}, u32[]{:S(2)}, u32[]{:S(2)}) async-start(bf16[4,128,512]{2,1,0:T(8,128)(2,1)} %bitcast.99), calls=%async_computation.4 | async-start | bytes 1048576 | tf_op jit(solution)/shard_map/all_to_all | solution.py:126
  105.1 2.8 %divide_convert_fusion = bf16[4,512,512]{1,2,0:T(8,128)(2,1)S(1)} fusion(f32[4,512,512]{1,2,0:T(8,128)} %get-tuple-element.54, f32[4,512]{1,0:T(4,128)S(1)} %get-tuple-element.53), kind=kLoop, calls=%fused_computation.2 | loop fusion | flops 2097152 | bytes 6299648 | tf_op jit(solution)/shard_map/while/body/eval_jaxpr/convert_element_type | solution.py:55
  107.9 2.0 %copy.50 = bf16[4,128,512]{2,1,0:T(8,128)(2,1)} copy(bf16[4,128,512]{1,2,0:T(8,128)(2,1)} %all_to_all.65) | data formatting | bytes 1048576 | tf_op jit(solution)/shard_map/all_to_all | solution.py:124
  109.9 2.0 %squeeze.14 = bf16[512,4,128]{2,1,0:T(4,128)(2,1)} reshape(bf16[4,128,512]{2,1,0:T(8,128)(2,1)} %copy.50) | data formatting | bytes 1048576 | tf_op jit(solution)/shard_map/while/body/jit(dynamic_index_in_dim)/squeeze | solution.py:148
  111.9 1.0 copy.55
  112.9 1.9 %reshape_squeeze.29 = bf16[512,4,128]{2,1,0:T(4,128)(2,1)} reshape(bf16[4,128,512]{2,1,0:T(8,128)(2,1)} %copy.55) | data formatting | bytes 1048576 | tf_op jit(solution)/shard_map/reshape;squeeze | solution.py:115
  114.9 1.2 reshape_squeeze.26
  116.0 2.0 %fusion.54 = (bf16[512,4,128]{2,0,1:T(8,128)(2,1)}, f32[512,4,128]{2,0,1:T(8,128)}) fusion(bf16[4,512,512]{1,2,0:T(8,128)(2,1)S(1)} %divide_convert_fusion, bf16[512,4,128]{2,1,0:T(4,128)(2,1)S(1)} %reshape_squeeze.26), kind=kOutput, calls=%fused_computation.83 | convolution fusion | flops 268697600 | bytes 4194304 | tf_op jit(solution)/shard_map/while/body/eval_jaxpr/hbk,khd->bhd/dot_general | solution.py:56
  118.1 2.7 %fusion.28 = f32[4,512,512]{1,2,0:T(8,128)} fusion(bf16[512,4,128]{2,1,0:T(4,128)(2,1)S(1)} %copy-done.8, bf16[512,4,128]{2,1,0:T(4,128)(2,1)S(1)} %reshape_squeeze.24), kind=kOutput, calls=%fused_computation.39 | convolution fusion | flops 268435456 | bytes 5242880 | tf_op jit(solution)/shard_map/while/body/eval_jaxpr/bhd,khd->hbk/dot_general | solution.py:64
  120.8 2.0 %reshape_squeeze.28 = bf16[512,4,128]{2,1,0:T(4,128)(2,1)} reshape(bf16[4,128,512]{2,1,0:T(8,128)(2,1)} %all-to-all-done.4) | data formatting | bytes 1048576 | tf_op jit(solution)/shard_map/reshape;squeeze | solution.py:115
  122.8 1.9 %fusion.30 = f32[4,512,128]{2,1,0:T(8,128)S(1)} fusion(bf16[4,512,512]{1,2,0:T(8,128)(2,1)S(1)} %divide_convert_fusion, bf16[512,4,128]{2,1,0:T(4,128)(2,1)} %reshape_squeeze.28), kind=kOutput, calls=%fused_computation.41 | convolution fusion | flops 268435456 | bytes 3670016 | tf_op jit(solution)/shard_map/while/body/eval_jaxpr/hbk,khd->bhd/dot_general | solution.py:71
  124.7 3.5 %fusion.55 = (f32[4,512]{1,0:T(4,128)S(1)}, bf16[4,512,512]{1,2,0:T(8,128)(2,1)S(1)}) fusion(f32[4,512,512]{1,2,0:T(8,128)} %fusion.28, bf16[512,4,128]{2,1,0:T(4,128)(2,1)} %reshape_squeeze.29, bf16[512,4,128]{2,1,0:T(4,128)(2,1)S(1)} %copy-done.3, bf16[4,512,512]{1,2,0:T(8,128)(2,1)S(1)} %divide_convert_fusion), kind=kOutput, calls=%fused_computation.84 | convolution fusion | flops 274724864 | bytes 9445376 | tf_op jit(solution)/shard_map/while/body/eval_jaxpr/bhd,khd->hbk/dot_general | solution.py:65
  128.2 0.9 fusion.16
  129.1 0.4 copy.60
  129.5 1.0 reshape.425
  130.5 4.9 %all-to-all-start.7 = ((bf16[4,128,512]{2,1,0:T(8,128)(2,1)}), bf16[4,128,512]{2,1,0:T(8,128)(2,1)S(1)}, u32[]{:S(2)}, u32[]{:S(2)}) async-start(bf16[4,128,512]{2,1,0:T(8,128)(2,1)} %reshape.425), calls=%async_computation.7 | async-start | bytes 1048576 | tf_op jit(solution)/shard_map/all_to_all | solution.py:155
  135.4 0.4 copy.43
  135.8 1.0 reshape.422
  136.8 12.1 %all-to-all-done.7 = bf16[4,128,512]{2,1,0:T(8,128)(2,1)S(1)} async-done(((bf16[4,128,512]{2,1,0:T(8,128)(2,1)}), bf16[4,128,512]{2,1,0:T(8,128)(2,1)S(1)}, u32[]{:S(2)}, u32[]{:S(2)}) %all-to-all-start.7) | async-done | bytes 524320 | tf_op jit(solution)/shard_map/all_to_all | solution.py:155
  148.9 3.5 %all-to-all-start.3 = ((bf16[4,128,512]{2,1,0:T(8,128)(2,1)}), bf16[4,128,512]{2,1,0:T(8,128)(2,1)S(1)}, u32[]{:S(2)}, u32[]{:S(2)}) async-start(bf16[4,128,512]{2,1,0:T(8,128)(2,1)} %reshape.422), calls=%async_computation.3 | async-start | bytes 1048576 | tf_op jit(solution)/shard_map/all_to_all | solution.py:154
  152.6 1.0 copy.63
  153.7 12.7 %all-to-all-done.3 = bf16[4,128,512]{2,1,0:T(8,128)(2,1)S(1)} async-done(((bf16[4,128,512]{2,1,0:T(8,128)(2,1)}), bf16[4,128,512]{2,1,0:T(8,128)(2,1)S(1)}, u32[]{:S(2)}, u32[]{:S(2)}) %all-to-all-start.3) | async-done | bytes 524320 | tf_op jit(solution)/shard_map/all_to_all | solution.py:154
  166.6 1.0 copy.62
  (49 shorter events, 3.6 us)
Async XLA Ops:
  0.6 2.8 %copy-start.11 = (bf16[1,128,2048]{2,1,0:T(8,128)(2,1)S(1)}, bf16[1,128,2048]{2,1,0:T(8,128)(2,1)}, u32[]{:S(2)}) copy-start(bf16[1,128,2048]{2,1,0:T(8,128)(2,1)} %param.7) | copy-start | bytes 1572868
  5.6 2.0 %copy-start.5 = (f32[128,16,127]{0,2,1:T(8,128)S(1)}, f32[128,16,127]{0,2,1:T(8,128)}, u32[]{:S(2)}) copy-start(f32[128,16,127]{0,2,1:T(8,128)} %get-tuple-element.46) | copy-start | bytes 3121156
  8.4 1.8 %copy-start = (f32[128,16,128]{0,2,1:T(8,128)}, f32[128,16,128]{0,2,1:T(8,128)S(1)}, u32[]{:S(2)}) copy-start(f32[128,16,128]{0,2,1:T(8,128)S(1)} %mul.164) | copy-start | bytes 3145732
  10.1 20.9 %all-to-all-start = ((bf16[4,128,512]{1,2,0:T(8,128)(2,1)}), bf16[4,128,512]{1,2,0:T(8,128)(2,1)}, u32[]{:S(2)}, u32[]{:S(2)}) async-start(bf16[4,128,512]{1,2,0:T(8,128)(2,1)} %get-tuple-element.25), calls=%async_computation | async-start | bytes 1048576 | tf_op jit(solution)/shard_map/all_to_all | solution.py:121
  20.4 1.2 copy-start.6
  20.5 1.5 copy-start.7
  22.0 1.2 copy-start.1
  25.0 47.1 %copy-start.12 = (bf16[1,128,2048]{2,1,0:T(8,128)(2,1)S(1)}, bf16[1,128,2048]{2,1,0:T(8,128)(2,1)}, u32[]{:S(2)}) copy-start(bf16[1,128,2048]{2,1,0:T(8,128)(2,1)} %param.12) | copy-start | bytes 1572868
  66.3 17.0 %all-to-all-start.6 = ((bf16[4,128,512]{1,2,0:T(8,128)(2,1)}), bf16[4,128,512]{1,2,0:T(8,128)(2,1)S(1)}, u32[]{:S(2)}, u32[]{:S(2)}) async-start(bf16[4,128,512]{1,2,0:T(8,128)(2,1)} %get-tuple-element.22), calls=%async_computation.6 | async-start | bytes 1048576 | tf_op jit(solution)/shard_map/all_to_all | solution.py:125
  74.7 12.8 %copy-start.2 = (bf16[512,4,128]{2,1,0:T(4,128)(2,1)}, bf16[512,4,128]{2,1,0:T(4,128)(2,1)S(1)}, u32[]{:S(2)}) copy-start(bf16[512,4,128]{2,1,0:T(4,128)(2,1)S(1)} %squeeze.13) | copy-start | bytes 1572868
  83.3 17.5 %all-to-all-start.2 = ((bf16[4,128,512]{2,1,0:T(8,128)(2,1)}), bf16[4,128,512]{2,1,0:T(8,128)(2,1)S(1)}, u32[]{:S(2)}, u32[]{:S(2)}) async-start(bf16[4,128,512]{2,1,0:T(8,128)(2,1)} %bitcast.100), calls=%async_computation.2 | async-start | bytes 1048576 | tf_op jit(solution)/shard_map/all_to_all | solution.py:123
  100.8 4.3 %copy-start.9 = (bf16[4,128,512]{2,1,0:T(8,128)(2,1)}, bf16[4,128,512]{2,1,0:T(8,128)(2,1)S(1)}, u32[]{:S(2)}) copy-start(bf16[4,128,512]{2,1,0:T(8,128)(2,1)S(1)} %all-to-all-done.2) | copy-start | bytes 1572868
  100.8 20.0 %all-to-all-start.4 = ((bf16[4,128,512]{2,1,0:T(8,128)(2,1)}), bf16[4,128,512]{2,1,0:T(8,128)(2,1)}, u32[]{:S(2)}, u32[]{:S(2)}) async-start(bf16[4,128,512]{2,1,0:T(8,128)(2,1)} %bitcast.99), calls=%async_computation.4 | async-start | bytes 1048576 | tf_op jit(solution)/shard_map/all_to_all | solution.py:126
  116.0 2.1 %copy-start.8 = (bf16[512,4,128]{2,1,0:T(4,128)(2,1)S(1)}, bf16[512,4,128]{2,1,0:T(4,128)(2,1)}, u32[]{:S(2)}) copy-start(bf16[512,4,128]{2,1,0:T(4,128)(2,1)} %squeeze.14) | copy-start | bytes 1572868
  120.7 4.0 %copy-start.3 = (bf16[512,4,128]{2,1,0:T(4,128)(2,1)S(1)}, bf16[512,4,128]{2,1,0:T(4,128)(2,1)}, u32[]{:S(2)}) copy-start(bf16[512,4,128]{2,1,0:T(4,128)(2,1)} %copy-done.2) | copy-start | bytes 1572868
  124.7 3.5 %copy-start.4 = (f32[512,4,128]{2,0,1:T(8,128)S(1)}, f32[512,4,128]{2,0,1:T(8,128)}, u32[]{:S(2)}) copy-start(f32[512,4,128]{2,0,1:T(8,128)} %get-tuple-element.56) | copy-start | bytes 3145732
  128.2 7.2 %copy-start.10 = (bf16[512,4,128]{2,0,1:T(8,128)(2,1)S(1)}, bf16[512,4,128]{2,0,1:T(8,128)(2,1)}, u32[]{:S(2)}) copy-start(bf16[512,4,128]{2,0,1:T(8,128)(2,1)} %get-tuple-element.55) | copy-start | bytes 1572868
  130.5 18.4 %all-to-all-start.7 = ((bf16[4,128,512]{2,1,0:T(8,128)(2,1)}), bf16[4,128,512]{2,1,0:T(8,128)(2,1)S(1)}, u32[]{:S(2)}, u32[]{:S(2)}) async-start(bf16[4,128,512]{2,1,0:T(8,128)(2,1)} %reshape.425), calls=%async_computation.7 | async-start | bytes 1048576 | tf_op jit(solution)/shard_map/all_to_all | solution.py:155
  148.9 17.5 %all-to-all-start.3 = ((bf16[4,128,512]{2,1,0:T(8,128)(2,1)}), bf16[4,128,512]{2,1,0:T(8,128)(2,1)S(1)}, u32[]{:S(2)}, u32[]{:S(2)}) async-start(bf16[4,128,512]{2,1,0:T(8,128)(2,1)} %reshape.422), calls=%async_computation.3 | async-start | bytes 1048576 | tf_op jit(solution)/shard_map/all_to_all | solution.py:154
where the time goes:
time: 169 us; the launch traced here: 168 us
  waiting for transfers between devices  49.3 us (29%)
  blocking collectives  35.2 us (21%)
  local copies, waits for them, and re-layouts  31.4 us (19%)
  starting transfers between devices  25.9 us (15%)
  other arithmetic  12.5 us (7%)
  matrix products  11.7 us (7%)
    all_to_all x1, blocking collectives, body(): lax.all_to_all(qdot_send, 'seq', split_axis=0, concat_axis=1, tiled=True)  17.7 us
    all_to_all x1, blocking collectives, body(): lax.all_to_all(key_send, 'seq', split_axis=0, concat_axis=1, tiled=True)  17.5 us
    all_to_all x1, waiting for transfers between devices, body(): lax.all_to_all(to_sources(attended), 'seq', split_axis=0, concat_axis=0,...  12.7 us
    all_to_all x1, waiting for transfers between devices, body(): lax.all_to_all(to_sources(tangent_out), 'seq', split_axis=0, concat_axis=...  12.1 us
    all_to_all x1, waiting for transfers between devices, body(): lax.all_to_all(value_send, 'seq', split_axis=0, concat_axis=1, tiled=True)  10.2 us
    all_to_all x1, waiting for transfers between devices, body(): lax.all_to_all(kdot_send, 'seq', split_axis=0, concat_axis=1, tiled=True)  8.22 us
    all_to_all x1, starting transfers between devices, body(): lax.all_to_all(query_send, 'seq', split_axis=0, concat_axis=1, tiled=True)  6.35 us
    all_to_all x1, waiting for transfers between devices, body(): lax.all_to_all(query_send, 'seq', split_axis=0, concat_axis=1, tiled=True)  6.11 us
  transfers between devices with their start and end apart: 6, of which 5 were waited for; matrix products, arithmetic and copies ran while one was open for 20% of the time, Pallas kernels for 0%

commit v1 on v0

--- a/solution.py
+++ b/solution.py
@@ -9,6 +9,15 @@
 HH = 44
 WW = 80
 rope_theta = 10000.0
+
+
+def _view_body(x_local, mesh_name):
+    v_now = lax.axis_size(mesh_name)
+    work_now = jnp.split(x_local, v_now, axis=0)
+    z2 = jnp.stack(work_now, axis=0)
+    block_next = lax.all_to_all(z2, mesh_name, 0, 0)
+    current_value = jnp.concatenate(block_next, axis=1)
+    return current_value
 
 
 def rope_tables(first, count):
@@ -119,7 +128,7 @@
 
     received = (
         lax.all_to_all(query_send, "seq", split_axis=0, concat_axis=1, tiled=True),
-        lax.all_to_all(key_send, "seq", split_axis=0, concat_axis=1, tiled=True),
+        _view_body(key_send, "seq"),
         lax.all_to_all(value_send, "seq", split_axis=0, concat_axis=1, tiled=True),
         lax.all_to_all(qdot_send, "seq", split_axis=0, concat_axis=1, tiled=True),
         lax.all_to_all(kdot_send, "seq", split_axis=0, concat_axis=1, tiled=True),

time: 169 us -> 162 us (0.959)
  blocking collectives: 35.2 us -> 0 us
  waiting for transfers between devices: 49.3 us -> 61.8 us
  starting transfers between devices: 25.9 us -> 33.6 us
  matrix products: 11.7 us -> 15.8 us
  other arithmetic: 12.5 us -> 16.2 us
    all_to_all x2 -> x0, blocking collectives: 35.2 us -> none  [the longest x1 17.7 us: body(): lax.all_to_all(qdot_send, 'seq', split_axis=0, concat_axis=1, tiled=True)]
    all_to_all x0 -> x2, waiting for transfers between devices: none -> 11.6 us  [the longest x1 7.19 us: _view_body(): block_next = lax.all_to_all(z2, mesh_name, 0, 0)]
    all_to_all x0 -> x2, starting transfers between devices: none -> 10.5 us  [the longest x1 6.35 us: _view_body(): block_next = lax.all_to_all(z2, mesh_name, 0, 0)]
    all_to_all x1, waiting for transfers between devices: 0.01 us -> 9.58 us  [body(): lax.all_to_all(vdot_send, 'seq', split_axis=0, concat_axis=1, tiled=True)]
    all_to_all x1, waiting for transfers between devices: 12.7 us -> 3.47 us  [body(): lax.all_to_all(to_sources(attended), 'seq', split_axis=0, concat_axis=0,...]
    all_to_all x1, waiting for transfers between devices: 8.22 us -> 0.01 us  [body(): lax.all_to_all(kdot_send, 'seq', split_axis=0, concat_axis=1, tiled=True)]
    all_to_all x1, waiting for transfers between devices: 6.11 us -> 11.7 us  [body(): lax.all_to_all(query_send, 'seq', split_axis=0, concat_axis=1, tiled=True)]
    sub x1, other arithmetic: 3.12 us -> 6.77 us  [primal_terms(): expons = jnp.exp(scores - largest)]
  transfers between devices with their start and end apart: 6 -> 8, of which waited for: 5 -> 7; matrix products, arithmetic and copies ran while one was open for 20% -> 32% of each run, Pallas kernels for 0% -> 0%
where the time goes in v1:
time: 162 us; the launch traced here: 161 us
  waiting for transfers between devices  61.8 us (38%)
  starting transfers between devices  33.6 us (21%)
  local copies, waits for them, and re-layouts  31.7 us (20%)
  other arithmetic  16.2 us (10%)
  matrix products  15.8 us (10%)
  between operations  1.67 us (1%)
    all_to_all x1, waiting for transfers between devices, body(): lax.all_to_all(value_send, 'seq', split_axis=0, concat_axis=1, tiled=True)  12.7 us
    all_to_all x1, waiting for transfers between devices, body(): lax.all_to_all(to_sources(tangent_out), 'seq', split_axis=0, concat_axis=...  12.7 us
    all_to_all x1, waiting for transfers between devices, body(): lax.all_to_all(query_send, 'seq', split_axis=0, concat_axis=1, tiled=True)  11.7 us
    all_to_all x1, waiting for transfers between devices, body(): lax.all_to_all(vdot_send, 'seq', split_axis=0, concat_axis=1, tiled=True)  9.58 us
    unnamed x24, local copies, waits for them, and re-layouts  7.34 us
    all_to_all x1, waiting for transfers between devices, _view_body(): block_next = lax.all_to_all(z2, mesh_name, 0, 0)  7.19 us
    sub x1, other arithmetic, primal_terms(): expons = jnp.exp(scores - largest)  6.77 us
    all_to_all x1, starting transfers between devices, _view_body(): block_next = lax.all_to_all(z2, mesh_name, 0, 0)  6.35 us
  transfers between devices with their start and end apart: 8, of which 7 were waited for; matrix products, arithmetic and copies ran while one was open for 32% of the time, Pallas kernels for 0%

profile of v1, /device:TPU:0, one launch (start us, length us, event | category | flops | bytes accessed | tf_op | source)
XLA Modules:
  0.0 160.8 jit_solution(4751909039980327634)
XLA Ops:
  1.4 1.3 copy.55
  3.0 2.0 %copy.36 = bf16[1,128,2048]{1,2,0:T(8,128)(2,1)} copy(bf16[1,128,2048]{2,1,0:T(8,128)(2,1)} %param.8) | data formatting | bytes 1048576 | tf_op args[1]
  5.0 1.1 convert_element_type.162
  7.5 1.5 fusion.25
  9.0 0.9 pad_maximum_fusion.4
  9.9 6.3 %all-to-all-start.1 = ((bf16[4,1,128,512]{2,3,1,0:T(8,128)(2,1)}), bf16[4,1,128,512]{2,3,1,0:T(8,128)(2,1)}, u32[]{:S(2)}, u32[]{:S(2)}) async-start(bf16[4,1,128,512]{2,3,1,0:T(8,128)(2,1)} %pad_maximum_fusion.4), calls=%async_computation.1 | async-start | bytes 1048576 | tf_op jit(solution)/shard_map/all_to_all | solution.py:18
  16.4 1.5 fusion.48
  17.9 1.2 copy.33
  19.4 1.0 copy-done.5
  21.3 0.6 copy-done.1
  21.9 1.7 %fusion.24 = (bf16[4,128,512]{1,2,0:T(8,128)(2,1)}, bf16[4,128,512]{1,2,0:T(8,128)(2,1)}) fusion(f32[1,128,4,512]{1,3,2,0:T(8,128)S(1)} %bitcast.131, f32[1,128,4,512]{1,3,2,0:T(8,128)S(1)} %bitcast.138, f32[1,128,4,512]{1,3,2,0:T(8,128)S(1)} %bitcast.139, f32[1,128,4,512]{1,3,2,0:T(8,128)S(1)} %bitcast.126, f32[1,128,4,512]{1,3,2,0:T(8,128)S(1)} %bitcast.133, ...), kind=kLoop, calls=%fused_computation.35 | loop fusion | flops 2621440 | bytes 9437696 | tf_op jit(solution)/shard_map/reshape | solution.py:106
  23.6 7.2 %all-to-all-done.1 = bf16[4,1,128,512]{2,3,1,0:T(8,128)(2,1)} async-done(((bf16[4,1,128,512]{2,3,1,0:T(8,128)(2,1)}), bf16[4,1,128,512]{2,3,1,0:T(8,128)(2,1)}, u32[]{:S(2)}, u32[]{:S(2)}) %all-to-all-start.1) | async-done | bytes 524320 | tf_op jit(solution)/shard_map/all_to_all | solution.py:18
  30.8 3.5 %all-to-all-start = ((bf16[4,128,512]{1,2,0:T(8,128)(2,1)}), bf16[4,128,512]{1,2,0:T(8,128)(2,1)S(1)}, u32[]{:S(2)}, u32[]{:S(2)}) async-start(bf16[4,128,512]{1,2,0:T(8,128)(2,1)} %get-tuple-element.25), calls=%async_computation | async-start | bytes 1048576 | tf_op jit(solution)/shard_map/all_to_all | solution.py:130
  34.3 1.4 reshape_squeeze.10
  35.7 0.9 copy.96
  36.6 11.7 %all-to-all-done = bf16[4,128,512]{1,2,0:T(8,128)(2,1)S(1)} async-done(((bf16[4,128,512]{1,2,0:T(8,128)(2,1)}), bf16[4,128,512]{1,2,0:T(8,128)(2,1)S(1)}, u32[]{:S(2)}, u32[]{:S(2)}) %all-to-all-start) | async-done | bytes 524320 | tf_op jit(solution)/shard_map/all_to_all | solution.py:130
  48.3 3.5 %all-to-all-start.2 = ((bf16[4,128,512]{2,1,0:T(8,128)(2,1)}), bf16[4,128,512]{2,1,0:T(8,128)(2,1)S(1)}, u32[]{:S(2)}, u32[]{:S(2)}) async-start(bf16[4,128,512]{2,1,0:T(8,128)(2,1)} %bitcast.112), calls=%async_computation.2 | async-start | bytes 1048576 | tf_op jit(solution)/shard_map/all_to_all | solution.py:132
  52.2 0.9 copy.95
  53.1 12.7 %all-to-all-done.2 = bf16[4,128,512]{2,1,0:T(8,128)(2,1)S(1)} async-done(((bf16[4,128,512]{2,1,0:T(8,128)(2,1)}), bf16[4,128,512]{2,1,0:T(8,128)(2,1)S(1)}, u32[]{:S(2)}, u32[]{:S(2)}) %all-to-all-start.2) | async-done | bytes 524320 | tf_op jit(solution)/shard_map/all_to_all | solution.py:132
  65.8 3.5 %all-to-all-start.4 = ((bf16[4,128,512]{2,1,0:T(8,128)(2,1)}), bf16[4,128,512]{2,1,0:T(8,128)(2,1)S(1)}, u32[]{:S(2)}, u32[]{:S(2)}) async-start(bf16[4,128,512]{2,1,0:T(8,128)(2,1)} %bitcast.111), calls=%async_computation.4 | async-start | bytes 1048576 | tf_op jit(solution)/shard_map/all_to_all | solution.py:135
  69.3 1.2 copy.39
  71.0 2.7 %fusion.35 = f32[4,512,512]{1,2,0:T(8,128)} fusion(bf16[512,4,128]{2,1,0:T(4,128)(2,1)S(1)} %reshape_squeeze_reshape.3, bf16[512,4,128]{2,1,0:T(4,128)(2,1)S(1)} %squeeze.13), kind=kOutput, calls=%fused_computation.49 | convolution fusion | flops 268435456 | bytes 5242880 | tf_op jit(solution)/shard_map/while/body/eval_jaxpr/bhd,khd->hbk/dot_general | solution.py:58
  73.7 9.6 %all-to-all-done.4 = bf16[4,128,512]{2,1,0:T(8,128)(2,1)S(1)} async-done(((bf16[4,128,512]{2,1,0:T(8,128)(2,1)}), bf16[4,128,512]{2,1,0:T(8,128)(2,1)S(1)}, u32[]{:S(2)}, u32[]{:S(2)}) %all-to-all-start.4) | async-done | bytes 524320 | tf_op jit(solution)/shard_map/all_to_all | solution.py:135
  83.3 4.1 %all-to-all-start.5 = ((bf16[4,128,512]{1,2,0:T(8,128)(2,1)}), bf16[4,128,512]{1,2,0:T(8,128)(2,1)}, u32[]{:S(2)}, u32[]{:S(2)}) async-start(bf16[4,128,512]{1,2,0:T(8,128)(2,1)} %get-tuple-element.24), calls=%async_computation.5 | async-start | bytes 1048576 | tf_op jit(solution)/shard_map/all_to_all | solution.py:133
  87.4 6.8 %fusion.53 = (f32[4,512]{1,0:T(4,128)S(1)}, f32[4,512,512]{1,2,0:T(8,128)}) fusion(f32[4,512,512]{1,2,0:T(8,128)} %fusion.35), kind=kOutput, calls=%fused_computation.87 | output fusion | flops 4194815 | bytes 8396800 | tf_op jit(solution)/shard_map/while/body/eval_jaxpr/sub | solution.py:62
  94.3 2.8 %divide_convert_fusion = bf16[4,512,512]{1,2,0:T(8,128)(2,1)S(1)} fusion(f32[4,512,512]{1,2,0:T(8,128)} %get-tuple-element.58, f32[4,512]{1,0:T(4,128)S(1)} %get-tuple-element.57), kind=kLoop, calls=%fused_computation.2 | loop fusion | flops 2097152 | bytes 6299648 | tf_op jit(solution)/shard_map/while/body/eval_jaxpr/convert_element_type | solution.py:64
  97.1 4.4 %all-to-all-done.5 = bf16[4,128,512]{1,2,0:T(8,128)(2,1)} async-done(((bf16[4,128,512]{1,2,0:T(8,128)(2,1)}), bf16[4,128,512]{1,2,0:T(8,128)(2,1)}, u32[]{:S(2)}, u32[]{:S(2)}) %all-to-all-start.5) | async-done | bytes 524320 | tf_op jit(solution)/shard_map/all_to_all | solution.py:133
  101.5 4.3 %all-to-all-start.6 = ((bf16[4,128,512]{1,2,0:T(8,128)(2,1)}), bf16[4,128,512]{1,2,0:T(8,128)(2,1)}, u32[]{:S(2)}, u32[]{:S(2)}) async-start(bf16[4,128,512]{1,2,0:T(8,128)(2,1)} %get-tuple-element.22), calls=%async_computation.6 | async-start | bytes 1048576 | tf_op jit(solution)/shard_map/all_to_all | solution.py:134
  105.9 1.9 %fusion.54 = (bf16[512,4,128]{2,0,1:T(8,128)(2,1)S(1)}, f32[512,4,128]{2,0,1:T(8,128)}) fusion(bf16[4,512,512]{1,2,0:T(8,128)(2,1)S(1)} %divide_convert_fusion, bf16[512,4,128]{2,1,0:T(4,128)(2,1)S(1)} %reshape_squeeze.22), kind=kOutput, calls=%fused_computation.88 | convolution fusion | flops 268697600 | bytes 4194304 | tf_op jit(solution)/shard_map/while/body/eval_jaxpr/hbk,khd->bhd/dot_general | solution.py:65
  107.8 1.2 copy.45
  109.0 2.0 %reshape.418 = bf16[4,128,512]{2,1,0:T(8,128)(2,1)} reshape(bf16[512,4,128]{2,1,0:T(4,128)(2,1)} %copy.45) | data formatting | bytes 1048576 | tf_op jit(solution)/shard_map/reshape | solution.py:160
  111.0 2.0 %copy.52 = bf16[4,128,512]{2,1,0:T(8,128)(2,1)} copy(bf16[4,128,512]{1,2,0:T(8,128)(2,1)} %all-to-all-done.5) | data formatting | bytes 1048576 | tf_op jit(solution)/shard_map/all_to_all | solution.py:133
  113.1 1.9 %squeeze.14 = bf16[512,4,128]{2,1,0:T(4,128)(2,1)} reshape(bf16[4,128,512]{2,1,0:T(8,128)(2,1)} %copy.52) | data formatting | bytes 1048576 | tf_op jit(solution)/shard_map/while/body/jit(dynamic_index_in_dim)/squeeze | solution.py:157
  115.0 2.0 %reshape_squeeze.24 = bf16[512,4,128]{2,1,0:T(4,128)(2,1)} reshape(bf16[4,128,512]{2,1,0:T(8,128)(2,1)} %copy-done.7) | data formatting | bytes 1048576 | tf_op jit(solution)/shard_map/reshape;squeeze | solution.py:124
  117.0 2.9 %fusion.30 = f32[4,512,128]{2,1,0:T(8,128)} fusion(bf16[4,512,512]{1,2,0:T(8,128)(2,1)S(1)} %divide_convert_fusion, bf16[512,4,128]{2,1,0:T(4,128)(2,1)} %reshape_squeeze.24), kind=kOutput, calls=%fused_computation.42 | convolution fusion | flops 268435456 | bytes 3670016 | tf_op jit(solution)/shard_map/while/body/eval_jaxpr/hbk,khd->bhd/dot_general | solution.py:80
  119.9 3.7 %fusion.28 = f32[4,512,512]{1,2,0:T(8,128)} fusion(bf16[512,4,128]{2,1,0:T(4,128)(2,1)} %squeeze.14, bf16[512,4,128]{2,1,0:T(4,128)(2,1)S(1)} %reshape_squeeze_reshape.3), kind=kOutput, calls=%fused_computation.40 | convolution fusion | flops 268435456 | bytes 5242880 | tf_op jit(solution)/shard_map/while/body/eval_jaxpr/bhd,khd->hbk/dot_general | solution.py:73
  123.7 4.9 %all-to-all-start.3 = ((bf16[4,128,512]{2,1,0:T(8,128)(2,1)}), bf16[4,128,512]{2,1,0:T(8,128)(2,1)S(1)}, u32[]{:S(2)}, u32[]{:S(2)}) async-start(bf16[4,128,512]{2,1,0:T(8,128)(2,1)} %reshape.418), calls=%async_computation.3 | async-start | bytes 1048576 | tf_op jit(solution)/shard_map/all_to_all | solution.py:163
  128.5 2.0 %copy.56 = bf16[4,128,512]{2,1,0:T(8,128)(2,1)} copy(bf16[4,128,512]{1,2,0:T(8,128)(2,1)} %all-to-all-done.6) | data formatting | bytes 1048576 | tf_op jit(solution)/shard_map/all_to_all | solution.py:134
  130.6 2.0 %reshape_squeeze.25 = bf16[512,4,128]{2,1,0:T(4,128)(2,1)} reshape(bf16[4,128,512]{2,1,0:T(8,128)(2,1)} %copy.56) | data formatting | bytes 1048576 | tf_op jit(solution)/shard_map/reshape;squeeze | solution.py:124
  132.5 3.7 %fusion.55 = (f32[4,512]{1,0:T(4,128)S(1)}, bf16[4,512,512]{1,2,0:T(8,128)(2,1)S(1)}) fusion(f32[4,512,512]{1,2,0:T(8,128)} %fusion.28, bf16[512,4,128]{2,1,0:T(4,128)(2,1)} %reshape_squeeze.25, bf16[512,4,128]{2,1,0:T(4,128)(2,1)} %copy-done.2, bf16[4,512,512]{1,2,0:T(8,128)(2,1)S(1)} %divide_convert_fusion), kind=kOutput, calls=%fused_computation.89 | convolution fusion | flops 274724864 | bytes 9445376 | tf_op jit(solution)/shard_map/while/body/eval_jaxpr/bhd,khd->hbk/dot_general | solution.py:74
  136.2 0.9 fusion.16
  137.1 0.4 copy.61
  137.5 1.0 reshape.421
  138.5 3.5 %all-to-all-done.3 = bf16[4,128,512]{2,1,0:T(8,128)(2,1)S(1)} async-done(((bf16[4,128,512]{2,1,0:T(8,128)(2,1)}), bf16[4,128,512]{2,1,0:T(8,128)(2,1)S(1)}, u32[]{:S(2)}, u32[]{:S(2)}) %all-to-all-start.3) | async-done | bytes 524320 | tf_op jit(solution)/shard_map/all_to_all | solution.py:163
  142.0 3.5 %all-to-all-start.7 = ((bf16[4,128,512]{2,1,0:T(8,128)(2,1)}), bf16[4,128,512]{2,1,0:T(8,128)(2,1)S(1)}, u32[]{:S(2)}, u32[]{:S(2)}) async-start(bf16[4,128,512]{2,1,0:T(8,128)(2,1)} %reshape.421), calls=%async_computation.7 | async-start | bytes 1048576 | tf_op jit(solution)/shard_map/all_to_all | solution.py:164
  145.8 1.0 copy.63
  146.8 12.7 %all-to-all-done.7 = bf16[4,128,512]{2,1,0:T(8,128)(2,1)S(1)} async-done(((bf16[4,128,512]{2,1,0:T(8,128)(2,1)}), bf16[4,128,512]{2,1,0:T(8,128)(2,1)S(1)}, u32[]{:S(2)}, u32[]{:S(2)}) %all-to-all-start.7) | async-done | bytes 524320 | tf_op jit(solution)/shard_map/all_to_all | solution.py:164
  159.8 1.0 copy.64
  (49 shorter events, 4.5 us)
Async XLA Ops:
  7.5 1.5 copy-start
  7.5 8.7 %copy-start.8 = (bf16[1,128,2048]{2,1,0:T(8,128)(2,1)S(1)}, bf16[1,128,2048]{2,1,0:T(8,128)(2,1)}, u32[]{:S(2)}) copy-start(bf16[1,128,2048]{2,1,0:T(8,128)(2,1)} %param.10) | copy-start | bytes 1572868
  9.9 20.9 %all-to-all-start.1 = ((bf16[4,1,128,512]{2,3,1,0:T(8,128)(2,1)}), bf16[4,1,128,512]{2,3,1,0:T(8,128)(2,1)}, u32[]{:S(2)}, u32[]{:S(2)}) async-start(bf16[4,1,128,512]{2,3,1,0:T(8,128)(2,1)} %pad_maximum_fusion.4), calls=%async_computation.1 | async-start | bytes 1048576 | tf_op jit(solution)/shard_map/all_to_all | solution.py:18
  19.2 1.2 copy-start.5
  19.2 1.5 copy-start.6
  20.7 1.2 copy-start.1
  23.6 28.2 %copy-start.9 = (bf16[1,128,2048]{2,1,0:T(8,128)(2,1)S(1)}, bf16[1,128,2048]{2,1,0:T(8,128)(2,1)}, u32[]{:S(2)}) copy-start(bf16[1,128,2048]{2,1,0:T(8,128)(2,1)} %param.12) | copy-start | bytes 1572868
  30.8 17.5 %all-to-all-start = ((bf16[4,128,512]{1,2,0:T(8,128)(2,1)}), bf16[4,128,512]{1,2,0:T(8,128)(2,1)S(1)}, u32[]{:S(2)}, u32[]{:S(2)}) async-start(bf16[4,128,512]{1,2,0:T(8,128)(2,1)} %get-tuple-element.25), calls=%async_computation | async-start | bytes 1048576 | tf_op jit(solution)/shard_map/all_to_all | solution.py:130
  48.3 17.5 %all-to-all-start.2 = ((bf16[4,128,512]{2,1,0:T(8,128)(2,1)}), bf16[4,128,512]{2,1,0:T(8,128)(2,1)S(1)}, u32[]{:S(2)}, u32[]{:S(2)}) async-start(bf16[4,128,512]{2,1,0:T(8,128)(2,1)} %bitcast.112), calls=%async_computation.2 | async-start | bytes 1048576 | tf_op jit(solution)/shard_map/all_to_all | solution.py:132
  65.8 17.5 %all-to-all-start.4 = ((bf16[4,128,512]{2,1,0:T(8,128)(2,1)}), bf16[4,128,512]{2,1,0:T(8,128)(2,1)S(1)}, u32[]{:S(2)}, u32[]{:S(2)}) async-start(bf16[4,128,512]{2,1,0:T(8,128)(2,1)} %bitcast.111), calls=%async_computation.4 | async-start | bytes 1048576 | tf_op jit(solution)/shard_map/all_to_all | solution.py:135
  71.0 16.4 %copy-start.2 = (bf16[512,4,128]{2,1,0:T(4,128)(2,1)}, bf16[512,4,128]{2,1,0:T(4,128)(2,1)S(1)}, u32[]{:S(2)}) copy-start(bf16[512,4,128]{2,1,0:T(4,128)(2,1)S(1)} %squeeze.13) | copy-start | bytes 1572868
  83.3 10.9 %copy-start.7 = (bf16[4,128,512]{2,1,0:T(8,128)(2,1)}, bf16[4,128,512]{2,1,0:T(8,128)(2,1)S(1)}, u32[]{:S(2)}) copy-start(bf16[4,128,512]{2,1,0:T(8,128)(2,1)S(1)} %all-to-all-done.4) | copy-start | bytes 1572868
  83.3 18.3 %all-to-all-start.5 = ((bf16[4,128,512]{1,2,0:T(8,128)(2,1)}), bf16[4,128,512]{1,2,0:T(8,128)(2,1)}, u32[]{:S(2)}, u32[]{:S(2)}) async-start(bf16[4,128,512]{1,2,0:T(8,128)(2,1)} %get-tuple-element.24), calls=%async_computation.5 | async-start | bytes 1048576 | tf_op jit(solution)/shard_map/all_to_all | solution.py:133
  101.5 22.1 %all-to-all-start.6 = ((bf16[4,128,512]{1,2,0:T(8,128)(2,1)}), bf16[4,128,512]{1,2,0:T(8,128)(2,1)}, u32[]{:S(2)}, u32[]{:S(2)}) async-start(bf16[4,128,512]{1,2,0:T(8,128)(2,1)} %get-tuple-element.22), calls=%async_computation.6 | async-start | bytes 1048576 | tf_op jit(solution)/shard_map/all_to_all | solution.py:134
  123.7 18.4 %all-to-all-start.3 = ((bf16[4,128,512]{2,1,0:T(8,128)(2,1)}), bf16[4,128,512]{2,1,0:T(8,128)(2,1)S(1)}, u32[]{:S(2)}, u32[]{:S(2)}) async-start(bf16[4,128,512]{2,1,0:T(8,128)(2,1)} %reshape.418), calls=%async_computation.3 | async-start | bytes 1048576 | tf_op jit(solution)/shard_map/all_to_all | solution.py:163
  132.5 3.7 %copy-start.3 = (f32[4,512,128]{2,1,0:T(8,128)S(1)}, f32[4,512,128]{2,1,0:T(8,128)}, u32[]{:S(2)}) copy-start(f32[4,512,128]{2,1,0:T(8,128)} %fusion.30) | copy-start | bytes 3145732
  132.5 3.7 %copy-start.4 = (f32[512,4,128]{2,0,1:T(8,128)S(1)}, f32[512,4,128]{2,0,1:T(8,128)}, u32[]{:S(2)}) copy-start(f32[512,4,128]{2,0,1:T(8,128)} %get-tuple-element.60) | copy-start | bytes 3145732
  142.0 17.5 %all-to-all-start.7 = ((bf16[4,128,512]{2,1,0:T(8,128)(2,1)}), bf16[4,128,512]{2,1,0:T(8,128)(2,1)S(1)}, u32[]{:S(2)}, u32[]{:S(2)}) async-start(bf16[4,128,512]{2,1,0:T(8,128)(2,1)} %reshape.421), calls=%async_computation.7 | async-start | bytes 1048576 | tf_op jit(solution)/shard_map/all_to_all | solution.py:164
